TPU v7x, 32 devices: a whole 2x2x4 slice. The times are simulated.
32 devices in a mesh: expert: 2 (over y), hidden: 4 (over z), dp: 4 (over x, core).
Axes of the slice: x: 2, y: 2, z: 4, core: 2. Of those that a mesh axis runs over, the one named last changes fastest.
Arguments:
- tokens: bfloat16 [2, 4, 512, 2048], P('expert', 'dp', None, 'hidden'), may hold values from -6 to 6
- grad_out: bfloat16 [2, 4, 512, 2048], P('expert', 'dp', None, 'hidden'), may hold values from -0.25 to 0.25
- gate_weight: bfloat16 [4, 2048, 512], P('expert', 'dp', 'hidden'), may hold values from -0.125 to 0.125
- up_weight: bfloat16 [4, 2048, 512], P('expert', 'dp', 'hidden'), may hold values from -0.125 to 0.125
- down_weight: bfloat16 [4, 512, 2048], P('expert', 'hidden', 'dp'), may hold values from -0.25 to 0.25
- matching: int32 [2], replicated, may hold values from 0 to 1, each once
- block_counts: int32 [2, 4, 2], P('expert', 'dp'), may hold values from 0 to 4, as said below
Outputs:
- grad_gate: bfloat16 [4, 2048, 512], P('expert', 'dp', 'hidden')
- grad_up: bfloat16 [4, 2048, 512], P('expert', 'dp', 'hidden')
- grad_down: bfloat16 [4, 512, 2048], P('expert', 'hidden', 'dp')
Inputs may be any that keep to these rules, and one draw needn't show every extreme that they name: `matching`: each expert index appears once. `block_counts`: the 2 counts of one expert index and data index sum to at most 4; on some device one count equals 4.
All inputs are finite; a program needn't handle non-finite values.
Results may differ from a plain program's by a relative error of at most 0.008.
Values may be sent and summed in bfloat16 or wider, within the bound.
A program may use at most 64 MiB of HBM per device.

v0:
```python
import jax
import jax.numpy as jnp
from jax import lax
from jax.sharding import PartitionSpec as P

BLOCK = 128


def contract_rows(left, right):
    return lax.dot_general(
        left, right, (((0,), (0,)), ((), ())), preferred_element_type=jnp.float32
    )


def block_owners(counts, blocks):
    bounds = jnp.cumsum(counts)
    index = jnp.arange(blocks, dtype=jnp.int32)
    owner = jnp.sum((index[:, None] >= bounds[None, :]).astype(jnp.int32), axis=1)
    owner = jnp.minimum(owner, counts.shape[0] - 1)
    alive = (index < bounds[-1]).astype(jnp.float32)
    return (owner, alive)


def add_into(total, term, expert):
    current = lax.dynamic_index_in_dim(total, expert, 0, keepdims=True)
    return lax.dynamic_update_index_in_dim(total, current + term[None], expert, 0)


def expert_terms(row_blocks, grad_blocks, weight_gate, weight_up, weight_down, owner, alive):
    zeros_gate = jnp.zeros(weight_gate.shape, jnp.float32)
    zeros_down = jnp.zeros(weight_down.shape, jnp.float32)

    def step(carry, inputs):
        total_gate, total_up, total_down = carry
        row_block, grad_block, expert, live = inputs
        gate_matrix = lax.dynamic_index_in_dim(weight_gate, expert, 0, keepdims=False)
        up_matrix = lax.dynamic_index_in_dim(weight_up, expert, 0, keepdims=False)
        down_matrix = lax.dynamic_index_in_dim(weight_down, expert, 0, keepdims=False)
        gate_value = jnp.dot(row_block, gate_matrix, preferred_element_type=jnp.float32)
        up_value = jnp.dot(row_block, up_matrix, preferred_element_type=jnp.float32)
        sigmoid_gate = jax.nn.sigmoid(gate_value)
        activated = gate_value * sigmoid_gate
        hidden = (activated * up_value * live).astype(jnp.bfloat16)
        grad_hidden = lax.dot_general(
            grad_block, down_matrix, (((1,), (1,)), ((), ())), preferred_element_type=jnp.float32
        )
        grad_gate = (
            grad_hidden * up_value * sigmoid_gate * (1.0 + gate_value * (1.0 - sigmoid_gate)) * live
        ).astype(jnp.bfloat16)
        grad_up = (grad_hidden * activated * live).astype(jnp.bfloat16)
        total_gate = add_into(total_gate, contract_rows(row_block, grad_gate), expert)
        total_up = add_into(total_up, contract_rows(row_block, grad_up), expert)
        total_down = add_into(total_down, contract_rows(hidden, grad_block), expert)
        return ((total_gate, total_up, total_down), None)

    totals, unused = lax.scan(
        step, (zeros_gate, zeros_gate, zeros_down), (row_blocks, grad_blocks, owner, alive)
    )
    return totals


def relocate(arrays, matching):
    groups = lax.axis_size("expert")
    joined = jnp.concatenate([array_piece.reshape(groups, -1) for array_piece in arrays], axis=1)
    spread = lax.all_to_all(joined, "expert", split_axis=0, concat_axis=0, tiled=True)
    ordered = jnp.take(spread, matching, axis=0)
    settled = lax.all_to_all(ordered, "expert", split_axis=0, concat_axis=0, tiled=True)
    pieces = []
    offset = 0
    for array_piece in arrays:
        length = array_piece.size // groups
        pieces.append(settled[:, offset : offset + length].reshape(array_piece.shape))
        offset = offset + length
    return pieces


def on_device(tokens, grad_out, gate_weight, up_weight, down_weight, matching, block_counts):
    moved = relocate((gate_weight, up_weight, down_weight), matching)
    weight_gate, weight_up, weight_down = (
        lax.all_gather(moved[0], "dp", axis=1, tiled=True),
        lax.all_gather(moved[1], "dp", axis=1, tiled=True),
        lax.all_gather(moved[2], "dp", axis=2, tiled=True),
    )
    rows_full, grads_full = (
        lax.all_gather(tokens[0, 0], "hidden", axis=1, tiled=True),
        lax.all_gather(grad_out[0, 0], "hidden", axis=1, tiled=True),
    )
    blocks = rows_full.shape[0] // BLOCK
    width = rows_full.shape[1]
    owner, alive = block_owners(block_counts[0, 0], blocks)
    totals = expert_terms(
        rows_full.reshape(blocks, BLOCK, width),
        grads_full.reshape(blocks, BLOCK, width),
        weight_gate,
        weight_up,
        weight_down,
        owner,
        alive,
    )
    summed = (
        lax.psum_scatter(
            totals[0].astype(jnp.bfloat16), "dp", scatter_dimension=1, tiled=True
        ).astype(jnp.float32),
        lax.psum_scatter(
            totals[1].astype(jnp.bfloat16), "dp", scatter_dimension=1, tiled=True
        ).astype(jnp.float32),
        lax.psum_scatter(
            totals[2].astype(jnp.bfloat16), "dp", scatter_dimension=2, tiled=True
        ).astype(jnp.float32),
    )
    return (
        summed[0].astype(jnp.bfloat16),
        summed[1].astype(jnp.bfloat16),
        summed[2].astype(jnp.bfloat16),
    )


def solution(mesh):
    in_specs = (
        P("expert", "dp", None, "hidden"),
        P("expert", "dp", None, "hidden"),
        P("expert", "dp", "hidden"),
        P("expert", "dp", "hidden"),
        P("expert", "hidden", "dp"),
        P(),
        P("expert", "dp", None),
    )
    out_specs = (
        P("expert", "dp", "hidden"),
        P("expert", "dp", "hidden"),
        P("expert", "hidden", "dp"),
    )
    return jax.shard_map(
        on_device, mesh=mesh, in_specs=in_specs, out_specs=out_specs, check_vma=False
    )
```

profile of v0, /device:TPU:0, one launch (start us, length us, event | category | flops | bytes accessed | tf_op | source)
XLA Modules:
  0.0 368.9 jit_solution(15848804387790991597)
XLA Ops:
  7.2 1.2 copy.19
  8.4 1.6 copy_bitcast_fusion.5
  10.0 9.9 %maximum_bitcast_fusion = bf16[2,1,196608]{2,0,1:T(2,128)(2,1)S(1)} fusion(bf16[2,65536]{1,0:T(2,128)(2,1)S(1)} %bitcast.118, bf16[2,65536]{1,0:T(2,128)(2,1)S(1)} %get-tuple-element.92, bf16[2,65536]{1,0:T(2,128)(2,1)S(1)} %get-tuple-element.93), kind=kLoop, calls=%fused_computation.51 | loop fusion | flops 2359296 | bytes 1572864 | tf_op jit(solution)/shard_map/all_to_all | solution.py:65
  20.4 2.6 reduce
  23.0 1.5 reshape.103
  24.5 4.3 %all-to-all-start = ((bf16[2,2,98304]{2,1,0:T(2,128)(2,1)}), bf16[2,2,98304]{2,1,0:T(2,128)(2,1)S(1)}, u32[]{:S(2)}, u32[]{:S(2)}) async-start(bf16[2,2,98304]{2,1,0:T(2,128)(2,1)} %reshape.103), calls=%async_computation | async-start | bytes 1572864 | tf_op jit(solution)/shard_map/all_to_all | solution.py:65
  28.8 11.5 %all-to-all-done = bf16[2,2,98304]{2,1,0:T(2,128)(2,1)S(1)} async-done(((bf16[2,2,98304]{2,1,0:T(2,128)(2,1)}), bf16[2,2,98304]{2,1,0:T(2,128)(2,1)S(1)}, u32[]{:S(2)}, u32[]{:S(2)}) %all-to-all-start) | async-done | bytes 786464 | tf_op jit(solution)/shard_map/all_to_all | solution.py:65
  40.3 0.7 reshape.104
  41.0 2.5 copy.31
  44.1 1.1 gather_fusion
  45.1 1.1 gather_fusion.1
  46.2 7.0 %broadcast_select_fusion = bf16[2,1,196608]{2,0,1:T(2,128)(2,1)S(1)} fusion(pred[2]{0:T(512)(128)(4,1)S(1)} %compare_and_fusion, bf16[2,98304]{1,0:T(2,128)(2,1)S(1)} %gather_fusion.1, bf16[2,98304]{1,0:T(2,128)(2,1)S(1)} %gather_fusion), kind=kLoop, calls=%fused_computation.50 | loop fusion | flops 1966080 | bytes 1572866 | tf_op jit(solution)/shard_map/jit(_take)/select_n | solution.py:66
  53.2 2.6 reduce.1
  56.4 12.9 %all_to_all.21 = bf16[2,2,98304]{2,1,0:T(2,128)(2,1)S(1)} all-to-all(bf16[2,2,98304]{2,1,0:T(2,128)(2,1)S(1)} %reshape.105), channel_id=1, replica_groups=mesh['expert'=2,'hidden'=4,'dp'=4] {'expert'}, dimensions={0} | all-to-all | bytes 1572864 | tf_op jit(solution)/shard_map/all_to_all | solution.py:67
  69.3 0.7 reshape.106
  70.0 2.5 copy.30
  73.1 0.7 copy.32
  73.9 0.7 copy.33
  74.7 0.7 copy.34
  78.3 12.6 %all-gather.12.cloned.1.call-done = bf16[2,2048,128]{2,1,0:T(8,128)(2,1)} async-done(((bf16[2,512,128]{2,1,0:T(8,128)(2,1)}), bf16[2,2048,128]{2,1,0:T(8,128)(2,1)}) %all-gather.12.cloned.1.call-update) | async-done | bytes 1048592 | tf_op jit(solution)/shard_map/all_gather | solution.py:80
  90.9 18.9 %all-gather.10.cloned.1.call-done = bf16[2,2048,128]{2,1,0:T(8,128)(2,1)} async-done(((bf16[2,512,128]{2,1,0:T(8,128)(2,1)}), bf16[2,2048,128]{2,1,0:T(8,128)(2,1)}) %all-gather.10.cloned.1.call-update) | async-done | bytes 1048592 | tf_op jit(solution)/shard_map/all_gather | solution.py:81
  109.8 18.9 %all-gather.8.cloned.1.call-done = bf16[2,128,2048]{2,1,0:T(8,128)(2,1)} async-done(((bf16[2,128,512]{2,1,0:T(8,128)(2,1)}), bf16[2,128,2048]{2,1,0:T(8,128)(2,1)}) %all-gather.8.cloned.1.call-update) | async-done | bytes 1048592 | tf_op jit(solution)/shard_map/all_gather | solution.py:82
  128.7 47.1 %all-gather.14.cloned.1.call-done = bf16[1,1,512,2048]{3,2,1,0:T(8,128)(2,1)} async-done(((bf16[1,1,512,512]{3,2,1,0:T(8,128)(2,1)}), bf16[1,1,512,2048]{3,2,1,0:T(8,128)(2,1)}) %all-gather.14.cloned.1.call-update) | async-done | bytes 2097168 | tf_op jit(solution)/shard_map/all_gather | solution.py:85
  175.8 45.9 %all-gather.16.cloned.1.call-done = bf16[1,1,512,2048]{3,2,1,0:T(8,128)(2,1)} async-done(((bf16[1,1,512,512]{3,2,1,0:T(8,128)(2,1)}), bf16[1,1,512,2048]{3,2,1,0:T(8,128)(2,1)}) %all-gather.16.cloned.1.call-update) | async-done | bytes 2097168 | tf_op jit(solution)/shard_map/all_gather | solution.py:86
  221.7 1.5 broadcast_in_dim.29.clone
  223.2 1.6 broadcast_in_dim.30
  224.8 1.4 broadcast_in_dim.29
  226.2 53.4 %while.14 = (s32[]{:T(128)}, f32[2,2048,128]{2,1,0:T(8,128)}, f32[2,2048,128]{2,1,0:T(8,128)}, f32[2,128,2048]{2,1,0:T(8,128)}, s32[4]{0:T(128)S(1)}, /*index=5*...) while((s32[]{:T(128)}, f32[2,2048,128]{2,1,0:T(8,128)}, ...), condition=%wide.region_3.4_spmd, body=%wide.region_2.3_spmd.sunk | while | flops 403849216 | bytes 61997988 | solution.py:56
  229.6 1.3 fusion.71
  231.0 1.7 fusion.70
  232.7 1.0 fusion.73
  233.7 1.2 fusion.72
  234.9 1.1 copy-done.4
  236.1 2.1 fusion.74
  238.2 1.3 copy-done.5
  242.1 0.6 dynamic_slice.103
  243.0 1.3 fusion.71
  244.3 1.6 fusion.70
  246.0 1.0 fusion.73
  247.1 1.2 fusion.72
  248.3 1.1 copy-done.4
  249.4 2.1 fusion.74
  251.6 1.3 copy-done.5
  255.5 0.6 dynamic_slice.103
  256.3 1.3 fusion.71
  257.7 1.7 fusion.70
  259.3 1.0 fusion.73
  260.4 1.2 fusion.72
  261.6 1.1 copy-done.4
  262.8 2.1 fusion.74
  264.9 1.3 copy-done.5
  269.7 1.3 fusion.71
  271.0 1.7 fusion.70
  272.7 1.0 fusion.73
  273.8 1.2 fusion.72
  275.0 1.1 copy-done.4
  276.1 2.1 fusion.74
  278.3 1.3 copy-done.5
  279.6 2.7 convert_element_type.34
  282.4 2.9 convert_element_type.32
  285.4 1.1 convert_element_type.33
  286.5 19.6 %reduce-scatter.8.cloned.1.call-done = bf16[2,128,512]{2,1,0:T(8,128)(2,1)} async-done(((bf16[2,128,2048]{2,1,0:T(8,128)(2,1)}), bf16[2,128,512]{2,1,0:T(8,128)(2,1)}) %reduce-scatter.8.cloned.1.call-update) | async-done | bytes 262160 | tf_op jit(solution)/shard_map/reduce_scatter | solution.py:107
  306.1 27.9 %reduce-scatter.4.cloned.1.call-done = bf16[2,512,128]{2,1,0:T(8,128)(2,1)} async-done(((bf16[2,2048,128]{2,1,0:T(8,128)(2,1)}), bf16[2,512,128]{2,1,0:T(8,128)(2,1)}) %reduce-scatter.4.cloned.1.call-update) | async-done | bytes 262160 | tf_op jit(solution)/shard_map/reduce_scatter | solution.py:101
  334.1 27.9 %reduce-scatter.6.cloned.1.call-done = bf16[2,512,128]{2,1,0:T(8,128)(2,1)} async-done(((bf16[2,2048,128]{2,1,0:T(8,128)(2,1)}), bf16[2,512,128]{2,1,0:T(8,128)(2,1)}) %reduce-scatter.6.cloned.1.call-update) | async-done | bytes 262160 | tf_op jit(solution)/shard_map/reduce_scatter | solution.py:104
  (88 shorter events, 10.0 us)
Async XLA Ops:
  20.4 8.4 %copy-start.9 = (s32[2]{0:T(128)S(1)}, s32[2]{0:T(128)}, u32[]{:S(2)}) copy-start(s32[2]{0:T(128)} %param.14) | copy-start | bytes 28
  24.5 15.8 %all-to-all-start = ((bf16[2,2,98304]{2,1,0:T(2,128)(2,1)}), bf16[2,2,98304]{2,1,0:T(2,128)(2,1)S(1)}, u32[]{:S(2)}, u32[]{:S(2)}) async-start(bf16[2,2,98304]{2,1,0:T(2,128)(2,1)} %reshape.103), calls=%async_computation | async-start | bytes 1572864 | tf_op jit(solution)/shard_map/all_to_all | solution.py:65
  28.8 62.2 %all-gather.12.cloned.1.call-start = ((), (), s32[]{:S(2)}) async-start(), calls=%async_computation.7 | async-start | bytes 1310720 | tf_op jit(solution)/shard_map/all_gather | solution.py:80
  73.1 3.8 %copy-start.10 = (s32[1,1,2]{2,1,0:T(1,128)S(1)}, s32[1,1,2]{2,1,0:T(1,128)}, u32[]{:S(2)}) copy-start(s32[1,1,2]{2,1,0:T(1,128)} %param.15) | copy-start | bytes 28
  73.8 36.0 %all-gather.10.cloned.1.call-start = ((), (), s32[]{:S(2)}) async-start(), calls=%async_computation.6 | async-start | bytes 1310720 | tf_op jit(solution)/shard_map/all_gather | solution.py:81
  74.6 54.0 %all-gather.8.cloned.1.call-start = ((), (), s32[]{:S(2)}) async-start(), calls=%async_computation.5 | async-start | bytes 1310720 | tf_op jit(solution)/shard_map/all_gather | solution.py:82
  75.4 100.3 %all-gather.14.cloned.1.call-start = ((), (), s32[]{:S(2)}) async-start(), calls=%async_computation.11 | async-start | bytes 2621440 | tf_op jit(solution)/shard_map/all_gather | solution.py:85
  76.0 145.7 %all-gather.16.cloned.1.call-start = ((), (), s32[]{:S(2)}) async-start(), calls=%async_computation.12 | async-start | bytes 2621440 | tf_op jit(solution)/shard_map/all_gather | solution.py:86
  76.6 229.5 %reduce-scatter.8.cloned.1.call-start = ((), (), s32[]{:S(2)}) async-start(), calls=%async_computation.10 | async-start | bytes 1310720 | tf_op jit(solution)/shard_map/reduce_scatter | solution.py:107
  223.2 3.1 copy-start
  223.2 3.1 copy-start.8
  228.8 3.9 %copy-start.1 = (f32[2,2048,128]{2,1,0:T(8,128)S(1)}, f32[2,2048,128]{2,1,0:T(8,128)}, u32[]{:S(2)}) copy-start(f32[2,2048,128]{2,1,0:T(8,128)} %get-tuple-element.177) | copy-start | bytes 6291460 | tf_op jit(solution)/shard_map/while
  231.0 2.7 copy-start.6
  233.7 4.5 %copy-start.2 = (f32[2,2048,128]{2,1,0:T(8,128)}, f32[2,2048,128]{2,1,0:T(8,128)S(1)}, u32[]{:S(2)}) copy-start(f32[2,2048,128]{2,1,0:T(8,128)S(1)} %fusion.73) | copy-start | bytes 6291460 | tf_op jit(solution)/shard_map/while
  233.7 2.4 copy-start.4
  236.1 2.1 copy-start.7
  238.2 1.4 copy-start.5
  242.1 3.9 %copy-start.1 = (f32[2,2048,128]{2,1,0:T(8,128)S(1)}, f32[2,2048,128]{2,1,0:T(8,128)}, u32[]{:S(2)}) copy-start(f32[2,2048,128]{2,1,0:T(8,128)} %get-tuple-element.177) | copy-start | bytes 6291460 | tf_op jit(solution)/shard_map/while
  244.3 2.7 copy-start.6
  247.1 4.5 %copy-start.2 = (f32[2,2048,128]{2,1,0:T(8,128)}, f32[2,2048,128]{2,1,0:T(8,128)S(1)}, u32[]{:S(2)}) copy-start(f32[2,2048,128]{2,1,0:T(8,128)S(1)} %fusion.73) | copy-start | bytes 6291460 | tf_op jit(solution)/shard_map/while
  247.1 2.4 copy-start.4
  249.4 2.1 copy-start.7
  251.6 1.4 copy-start.5
  255.4 3.9 %copy-start.1 = (f32[2,2048,128]{2,1,0:T(8,128)S(1)}, f32[2,2048,128]{2,1,0:T(8,128)}, u32[]{:S(2)}) copy-start(f32[2,2048,128]{2,1,0:T(8,128)} %get-tuple-element.177) | copy-start | bytes 6291460 | tf_op jit(solution)/shard_map/while
  257.7 2.7 copy-start.6
  260.4 4.5 %copy-start.2 = (f32[2,2048,128]{2,1,0:T(8,128)}, f32[2,2048,128]{2,1,0:T(8,128)S(1)}, u32[]{:S(2)}) copy-start(f32[2,2048,128]{2,1,0:T(8,128)S(1)} %fusion.73) | copy-start | bytes 6291460 | tf_op jit(solution)/shard_map/while
  260.4 2.4 copy-start.4
  262.8 2.1 copy-start.7
  264.9 1.4 copy-start.5
  268.8 3.9 %copy-start.1 = (f32[2,2048,128]{2,1,0:T(8,128)S(1)}, f32[2,2048,128]{2,1,0:T(8,128)}, u32[]{:S(2)}) copy-start(f32[2,2048,128]{2,1,0:T(8,128)} %get-tuple-element.177) | copy-start | bytes 6291460 | tf_op jit(solution)/shard_map/while
  271.0 2.7 copy-start.6
  273.7 4.5 %copy-start.2 = (f32[2,2048,128]{2,1,0:T(8,128)}, f32[2,2048,128]{2,1,0:T(8,128)S(1)}, u32[]{:S(2)}) copy-start(f32[2,2048,128]{2,1,0:T(8,128)S(1)} %fusion.73) | copy-start | bytes 6291460 | tf_op jit(solution)/shard_map/while
  273.8 2.4 copy-start.4
  276.1 2.1 copy-start.7
  278.3 1.4 copy-start.5
  282.4 51.7 %reduce-scatter.4.cloned.1.call-start = ((), (), s32[]{:S(2)}) async-start(), calls=%async_computation.8 | async-start | bytes 1310720 | tf_op jit(solution)/shard_map/reduce_scatter | solution.py:101
  282.4 2.9 copy-start.3
  285.3 76.7 %reduce-scatter.6.cloned.1.call-start = ((), (), s32[]{:S(2)}) async-start(), calls=%async_computation.9 | async-start | bytes 1310720 | tf_op jit(solution)/shard_map/reduce_scatter | solution.py:104
Sparse Core Ops, SparseCore 0:
  73.9 16.9 all-gather.11
  93.0 16.6 all-gather.9
  111.9 16.6 all-gather.7
  130.1 45.6 all-gather.13
  177.2 44.4 all-gather.15
  282.5 23.5 reduce-scatter.7
  309.2 24.8 reduce-scatter.3
  337.2 24.8 reduce-scatter.5
where the time goes:
time: 370 us; the launch traced here: 369 us
  waiting for transfers between devices  232 us (63%)
  local copies, waits for them, and re-layouts  36.9 us (10%)
  matrix products  30.5 us (8%)
  other arithmetic  29.7 us (8%)
  between operations  14.3 us (4%)
  blocking collectives  12.9 us (3%)
  loops' own time  8.17 us (2%)
  starting transfers between devices  4.77 us (1%)
    all_gather x1, waiting for transfers between devices, on_device(): lax.all_gather(tokens[0, 0], 'hidden', axis=1, tiled=True)  47.1 us
    all_gather x1, waiting for transfers between devices, on_device(): lax.all_gather(grad_out[0, 0], 'hidden', axis=1, tiled=True)  45.9 us
    reduce_scatter x1, waiting for transfers between devices, on_device(): lax.psum_scatter(totals[1].astype(jnp.bfloat16), 'dp', scatter_dimension=...  27.9 us
    reduce_scatter x1, waiting for transfers between devices, on_device(): lax.psum_scatter(totals[0].astype(jnp.bfloat16), 'dp', scatter_dimension=...  27.9 us
    reduce_scatter x1, waiting for transfers between devices, on_device(): lax.psum_scatter(totals[2].astype(jnp.bfloat16), 'dp', scatter_dimension=...  19.6 us
    all_gather x1, waiting for transfers between devices, on_device(): lax.all_gather(moved[2], 'dp', axis=2, tiled=True)  18.9 us
    all_gather x1, waiting for transfers between devices, on_device(): lax.all_gather(moved[1], 'dp', axis=1, tiled=True)  18.9 us
    dot_general x12, matrix products, contract_rows(): lax.dot_general(left, right, (((0,), (0,)), ((), ())), preferred_element_...  17.5 us
  transfers between devices with their start and end apart: 9, of which 9 were waited for; matrix products, arithmetic and copies ran while one was open for 2% of the time, Pallas kernels for 0%

commit v1 on v0

--- a/solution.py
+++ b/solution.py
@@ -1,6 +1,10 @@
+import functools
+
 import jax
 import jax.numpy as jnp
 from jax import lax
+from jax.experimental import pallas as pl
+from jax.experimental.pallas import tpu as pltpu
 from jax.sharding import PartitionSpec as P
 
 BLOCK = 128
@@ -74,7 +78,7 @@
     return pieces
 
 
-def on_device(tokens, grad_out, gate_weight, up_weight, down_weight, matching, block_counts):
+def on_device_plain(tokens, grad_out, gate_weight, up_weight, down_weight, matching, block_counts):
     moved = relocate((gate_weight, up_weight, down_weight), matching)
     weight_gate, weight_up, weight_down = (
         lax.all_gather(moved[0], "dp", axis=1, tiled=True),
@@ -115,7 +119,390 @@
     )
 
 
+MESH = pl.DeviceIdType.MESH
+TILE = 256
+
+
+def flip(index, bit):
+    return index + bit - 2 * bit * ((index // bit) % 2)
+
+
+def fused_kernel(
+    exchange, experts, counts_ref, match_ref, tok_ref, grad_ref, gate_ref, up_ref, down_ref,
+    out_gate, out_up, out_down,
+    tok_all, grad_all, gu_all, dn_all, old_gate, old_up, old_down,
+    acc_gu, acc_gh, pre, hid, gate_sel, up_sel,
+    part_gu, part_dn, core_gu, core_dn, sum_gu, sum_dn, far_gu, far_dn,
+    z_send, z_recv, y_send, y_recv, w_send, w_recv, r_send, r_recv,
+):
+    zs = lax.axis_size("hidden")
+    h = lax.axis_index("hidden")
+    d = lax.axis_index("dp")
+    p = lax.axis_index("expert")
+    rows, feats = tok_ref.shape
+    width = gate_ref.shape[2]
+    blocks = rows // BLOCK
+    near, far = flip(d, 1), flip(d, 2)
+    cross = flip(near, 2)
+
+    def remote(source, target, send, recv, where):
+        return pltpu.make_async_remote_copy(
+            src_ref=source, dst_ref=target, send_sem=send, recv_sem=recv,
+            device_id=where, device_id_type=MESH,
+        )
+
+    barrier = pltpu.get_barrier_semaphore()
+    for bit_partner in (near, far):
+        pl.semaphore_signal(barrier, inc=1, device_id={"dp": bit_partner}, device_id_type=MESH)
+    if exchange:
+        pl.semaphore_signal(barrier, inc=1, device_id={"expert": 1 - p}, device_id_type=MESH)
+
+    @pl.when(h > 0)
+    def _():
+        pl.semaphore_signal(barrier, inc=1, device_id={"hidden": h - 1}, device_id_type=MESH)
+
+    @pl.when(h < zs - 1)
+    def _():
+        pl.semaphore_signal(barrier, inc=1, device_id={"hidden": h + 1}, device_id_type=MESH)
+
+    peers = (h + zs - 1) // zs + (2 * zs - 2 - h) // zs
+    pl.semaphore_wait(barrier, peers + (3 if exchange else 2))
+
+    mine = (tok_ref, grad_ref)
+    whole = (tok_all, grad_all)
+
+    def line(kind, way, step, slab):
+        to = h + 1 if way == 0 else h - 1
+        source = mine[kind] if step == 0 else whole[kind].at[slab]
+        return remote(
+            source, whole[kind].at[slab], z_send.at[kind, way, step], z_recv.at[kind, way, step],
+            {"hidden": to},
+        )
+
+    def sends(way, step):
+        if way == 0:
+            return (h + 1 < zs) & (h - step >= 0), h - step
+        return (h - 1 >= 0) & (h + step < zs), h + step
+
+    def takes(way, step):
+        if way == 0:
+            return h - 1 - step >= 0, h - 1 - step
+        return h + 1 + step < zs, h + 1 + step
+
+    def line_start(kind, step):
+        for way in (0, 1):
+            valid, slab = sends(way, step)
+
+            @pl.when(valid)
+            def _():
+                line(kind, way, step, slab).start()
+
+    def line_finish(kind, step):
+        for way in (0, 1):
+            valid, slab = sends(way, step)
+
+            @pl.when(valid)
+            def _():
+                line(kind, way, step, slab).wait_send()
+
+    def line_take(kind, step):
+        for way in (0, 1):
+            valid, slab = takes(way, step)
+
+            @pl.when(valid)
+            def _():
+                line(kind, way, step, slab).wait_recv()
+        if step + 1 < zs - 1:
+            line_start(kind, step + 1)
+
+    def swap(i):
+        source = (gate_ref, up_ref, down_ref)[i]
+        target = (old_gate, old_up, old_down)[i]
+        return remote(source, target, y_send.at[i], y_recv.at[i], {"expert": 1 - p})
+
+    line_start(0, 0)
+    if exchange:
+        swap(0).start()
+        swap(1).start()
+    line_start(1, 0)
+    if exchange:
+        swap(2).start()
+
+    tok_all[h] = tok_ref[...]
+    grad_all[h] = grad_ref[...]
+
+    def chosen(own, other, e):
+        if not exchange:
+            return own[e]
+        return jnp.where(match_ref[p] == p, own[e], other[e])
+
+    weights = (gu_all, dn_all)
+
+    def spread(kind, i):
+        slab = (d, d, far)[i]
+        to = (far, near, near)[i]
+        ref = weights[kind].at[slab]
+        return remote(ref, ref, w_send.at[kind, i], w_recv.at[kind, i], {"dp": to})
+
+    def arrived(kind, i):
+        slab = (far, near, cross)[i]
+        ref = weights[kind].at[slab]
+        remote(ref, ref, w_send.at[kind, i], w_recv.at[kind, i], {"dp": near}).wait_recv()
+
+    if exchange:
+        swap(0).wait_recv()
+        swap(1).wait_recv()
+    for e in range(experts):
+        gu_all[d, e, :, :width] = chosen(gate_ref, old_gate, e)
+        gu_all[d, e, :, width:] = chosen(up_ref, old_up, e)
+    spread(0, 0).start()
+    spread(0, 1).start()
+    line_take(0, 0)
+    if exchange:
+        swap(2).wait_recv()
+    for e in range(experts):
+        dn_all[d, e * width : (e + 1) * width, :] = chosen(down_ref, old_down, e)
+    spread(1, 0).start()
+    spread(1, 1).start()
+    line_take(1, 0)
+    for kind in (0, 1):
+        arrived(kind, 0)
+        spread(kind, 2).start()
+    for kind in (0, 1):
+        arrived(kind, 1)
+        arrived(kind, 2)
+
+    def add_tokens(slab, first=False):
+        @pl.loop(0, rows // TILE)
+        def _(i):
+            part = pl.ds(pl.multiple_of(i * TILE, TILE), TILE)
+            for e in range(experts):
+                term = jnp.dot(tok_all[slab, part], gu_all[slab, e], preferred_element_type=jnp.float32)
+                acc_gu[e, part] = term if first else acc_gu[e, part] + term
+
+    def add_grads(slab, first=False):
+        @pl.loop(0, rows // TILE)
+        def _(i):
+            part = pl.ds(pl.multiple_of(i * TILE, TILE), TILE)
+            term = lax.dot_general(
+                grad_all[slab, part], dn_all[slab], (((1,), (1,)), ((), ())),
+                preferred_element_type=jnp.float32,
+            )
+            acc_gh[part] = term if first else acc_gh[part] + term
+
+    def add_step(kind, step):
+        for way in (0, 1):
+            valid, slab = takes(way, step)
+
+            @pl.when(valid)
+            def _():
+                (add_tokens, add_grads)[kind](slab)
+
+    add_tokens(h, True)
+    add_grads(h, True)
+    add_step(0, 0)
+    add_step(1, 0)
+    for step in range(1, zs - 2):
+        line_take(0, step)
+        add_step(0, step)
+        line_take(1, step)
+        add_step(1, step)
+    line_take(0, zs - 2)
+    add_step(0, zs - 2)
+
+    bounds = [counts_ref[0]]
+    for e in range(1, experts):
+        bounds.append(bounds[-1] + counts_ref[e])
+    picks, masks = [], []
+    for b in range(blocks):
+        owner = jnp.int32(0)
+        for e in range(experts):
+            owner = owner + jnp.where(b >= bounds[e], 1, 0)
+        owner = jnp.minimum(owner, experts - 1)
+        alive = jnp.where(b < bounds[-1], 1.0, 0.0)
+        picks.append([jnp.where(owner == e, 1.0, 0.0) for e in range(experts)])
+        masks.append([picks[b][e] * alive for e in range(experts)])
+
+    for b in range(blocks):
+        part = slice(b * BLOCK, (b + 1) * BLOCK)
+        both = sum(acc_gu[e, part] * picks[b][e] for e in range(experts))
+        gate_value, up_value = both[:, :width], both[:, width:]
+        gate_sel[part] = gate_value
+        up_sel[part] = up_value
+        hidden = (gate_value * jax.nn.sigmoid(gate_value) * up_value)
+        for e in range(experts):
+            hid[part, e * width : (e + 1) * width] = (hidden * masks[b][e]).astype(jnp.bfloat16)
+
+    line_take(1, zs - 2)
+    add_step(1, zs - 2)
+
+    def reduce_near(kind, i):
+        slab = (cross, near)[i]
+        source = (part_gu, part_dn)[kind].at[slab]
+        target = (core_gu, core_dn)[kind].at[i]
+        return remote(source, target, r_send.at[kind, i], r_recv.at[kind, i], {"dp": near})
+
+    def reduce_far(kind):
+        return remote(
+            (sum_gu, sum_dn)[kind], (far_gu, far_dn)[kind], r_send.at[kind, 2], r_recv.at[kind, 2],
+            {"dp": far},
+        )
+
+    def down_term(slab):
+        part_dn[slab] = lax.dot_general(
+            hid[...], grad_all[slab], (((0,), (0,)), ((), ())), preferred_element_type=jnp.float32
+        ).astype(jnp.bfloat16)
+
+    def gate_term(slab):
+        @pl.loop(0, feats // TILE)
+        def _(i):
+            part = pl.ds(pl.multiple_of(i * TILE, TILE), TILE)
+            part_gu[slab, part] = lax.dot_general(
+                tok_all[slab, :, part], pre[...], (((0,), (0,)), ((), ())),
+                preferred_element_type=jnp.float32,
+            ).astype(jnp.bfloat16)
+
+    def add_near(kind, i, slab):
+        own = (part_gu, part_dn)[kind]
+        got = (core_gu, core_dn)[kind]
+        return own[slab].astype(jnp.float32) + got[i].astype(jnp.float32)
+
+    def down_first():
+        down_term(cross)
+        reduce_near(1, 0).start()
+        down_term(far)
+        reduce_near(1, 0).wait_recv()
+        sum_dn[...] = add_near(1, 0, far).astype(jnp.bfloat16)
+        reduce_far(1).start()
+
+    def down_rest():
+        down_term(near)
+        reduce_near(1, 1).start()
+        down_term(d)
+
+    for b in range(blocks):
+        part = slice(b * BLOCK, (b + 1) * BLOCK)
+        gate_value, up_value = gate_sel[part], up_sel[part]
+        grad_hidden = sum(
+            acc_gh[part, e * width : (e + 1) * width] * picks[b][e] for e in range(experts)
+        )
+        s = jax.nn.sigmoid(gate_value)
+        grad_gate = grad_hidden * up_value * s * (1.0 + gate_value * (1.0 - s))
+        grad_up = grad_hidden * gate_value * s
+        for e in range(experts):
+            at = e * 2 * width
+            pre[part, at : at + width] = (grad_gate * masks[b][e]).astype(jnp.bfloat16)
+            pre[part, at + width : at + 2 * width] = (grad_up * masks[b][e]).astype(jnp.bfloat16)
+
+    gate_term(cross)
+    reduce_near(0, 0).start()
+    gate_term(far)
+    reduce_near(0, 0).wait_recv()
+    sum_gu[...] = add_near(0, 0, far).astype(jnp.bfloat16)
+    reduce_far(0).start()
+    down_first()
+    gate_term(near)
+    reduce_near(0, 1).start()
+    gate_term(d)
+    down_rest()
+
+    reduce_near(0, 1).wait_recv()
+    reduce_far(0).wait_recv()
+    total = add_near(0, 1, d) + far_gu[...].astype(jnp.float32)
+    for e in range(experts):
+        at = e * 2 * width
+        out_gate[e] = total[:, at : at + width].astype(jnp.bfloat16)
+        out_up[e] = total[:, at + width : at + 2 * width].astype(jnp.bfloat16)
+    reduce_near(1, 1).wait_recv()
+    reduce_far(1).wait_recv()
+    total = add_near(1, 1, d) + far_dn[...].astype(jnp.float32)
+    for e in range(experts):
+        out_down[e] = total[e * width : (e + 1) * width].astype(jnp.bfloat16)
+
+    for kind in (0, 1):
+        for step in range(zs - 1):
+            line_finish(kind, step)
+        for i in range(3):
+            spread(kind, i).wait_send()
+        for i in range(2):
+            reduce_near(kind, i).wait_send()
+        reduce_far(kind).wait_send()
+    if exchange:
+        for i in range(3):
+            swap(i).wait_send()
+
+
+def on_device_fused(tokens, grad_out, gate_weight, up_weight, down_weight, matching, block_counts):
+    groups = lax.axis_size("expert")
+    zs = lax.axis_size("hidden")
+    ds = lax.axis_size("dp")
+    exchange = groups == 2
+    if not exchange:
+        gate_weight, up_weight, down_weight = relocate(
+            (gate_weight, up_weight, down_weight), matching
+        )
+        matching = jnp.zeros_like(matching)
+    rows, feats = tokens.shape[2:]
+    experts, part, width = gate_weight.shape
+    vmem = pl.BlockSpec(memory_space=pltpu.VMEM)
+    smem = pl.BlockSpec(memory_space=pltpu.SMEM)
+    half, full = jnp.bfloat16, jnp.float32
+    wide = experts * 2 * width
+    tall = experts * width
+    dma = pltpu.SemaphoreType.DMA
+    return pl.pallas_call(
+        functools.partial(fused_kernel, exchange, experts),
+        out_shape=tuple(
+            jax.ShapeDtypeStruct(w.shape, half) for w in (gate_weight, up_weight, down_weight)
+        ),
+        in_specs=[smem, smem] + [vmem] * 5,
+        out_specs=(vmem,) * 3,
+        scratch_shapes=[
+            pltpu.VMEM((zs, rows, feats), half),
+            pltpu.VMEM((zs, rows, feats), half),
+            pltpu.VMEM((ds, experts, part, 2 * width), half),
+            pltpu.VMEM((ds, tall, part), half),
+            pltpu.VMEM(gate_weight.shape, half),
+            pltpu.VMEM(up_weight.shape, half),
+            pltpu.VMEM(down_weight.shape, half),
+            pltpu.VMEM((experts, rows, 2 * width), full),
+            pltpu.VMEM((rows, tall), full),
+            pltpu.VMEM((rows, wide), half),
+            pltpu.VMEM((rows, tall), half),
+            pltpu.VMEM((rows, width), full),
+            pltpu.VMEM((rows, width), full),
+            pltpu.VMEM((ds, part, wide), half),
+            pltpu.VMEM((ds, tall, part), half),
+            pltpu.VMEM((2, part, wide), half),
+            pltpu.VMEM((2, tall, part), half),
+            pltpu.VMEM((part, wide), half),
+            pltpu.VMEM((tall, part), half),
+            pltpu.VMEM((part, wide), half),
+            pltpu.VMEM((tall, part), half),
+            dma((2, 2, zs - 1)),
+            dma((2, 2, zs - 1)),
+            dma((3,)),
+            dma((3,)),
+            dma((2, 3)),
+            dma((2, 3)),
+            dma((2, 3)),
+            dma((2, 3)),
+        ],
+        compiler_params=pltpu.CompilerParams(
+            collective_id=0, has_side_effects=True, vmem_limit_bytes=48 * 1024 * 1024
+        ),
+    )(
+        block_counts.reshape(-1), matching, tokens.reshape(rows, feats),
+        grad_out.reshape(rows, feats), gate_weight, up_weight, down_weight,
+    )
+
+
+def fused_fits(mesh):
+    return mesh.shape["dp"] == 4 and mesh.shape["hidden"] == 4
+
+
 def solution(mesh):
+    on_device = on_device_fused if fused_fits(mesh) else on_device_plain
     in_specs = (
         P("expert", "dp", None, "hidden"),
         P("expert", "dp", None, "hidden"),

time: 370 us -> 104 us (0.28)
  waiting for transfers between devices: 232 us -> 0 us
  Pallas kernels: 0 us -> 95.3 us
  matrix products: 30.5 us -> 0 us
  other arithmetic: 29.7 us -> 0 us
  local copies, waits for them, and re-layouts: 36.9 us -> 7.7 us
  between operations: 14.3 us -> 0.66 us
  blocking collectives: 12.9 us -> 0 us
  loops' own time: 8.17 us -> 0 us
  starting transfers between devices: 4.77 us -> 0 us
    all_gather x5 -> x0, waiting for transfers between devices: 143 us -> none  [the longest x1 47.1 us: on_device(): lax.all_gather(tokens[0, 0], 'hidden', axis=1, tiled=True)]
    pallas_call x0 -> x1, Pallas kernels: none -> 95.3 us  [on_device_fused(): pl.pallas_call(functools.partial(fused_kernel, exchange, experts), out_sh...]
    reduce_scatter x3 -> x0, waiting for transfers between devices: 75.5 us -> none  [the longest x1 27.9 us: on_device(): lax.psum_scatter(totals[1].astype(jnp.bfloat16), 'dp', scatter_dimension=...]
    dot_general x24 -> x0, matrix products: 30.5 us -> none  [the longest x12 17.5 us: contract_rows(): lax.dot_general(left, right, (((0,), (0,)), ((), ())), preferred_element_...]
    all_to_all x1 -> x0, blocking collectives: 12.9 us -> none  [relocate(): lax.all_to_all(ordered, 'expert', split_axis=0, concat_axis=0, tiled=True)]
    all_to_all x2 -> x0, other arithmetic: 12.5 us -> none  [relocate(): lax.all_to_all(joined, 'expert', split_axis=0, concat_axis=0, tiled=True)]
    all_to_all x1 -> x0, waiting for transfers between devices: 11.5 us -> none  [relocate(): lax.all_to_all(joined, 'expert', split_axis=0, concat_axis=0, tiled=True)]
    while x48 -> x0, local copies, waits for them, and re-layouts: 10 us -> none
  transfers between devices with their start and end apart: 9 -> 0, of which waited for: 9 -> 0; matrix products, arithmetic and copies ran while one was open for 2% -> 0% of each run, Pallas kernels for 0% -> 0%
where the time goes in v1:
time: 104 us
  Pallas kernels  95.3 us (92%)
  local copies, waits for them, and re-layouts  7.7 us (7%)
    pallas_call x1, Pallas kernels, on_device_fused(): pl.pallas_call(functools.partial(fused_kernel, exchange, experts), out_sh...  95.3 us
    unnamed x17, local copies, waits for them, and re-layouts  7.7 us

profile of v1, /device:TPU:0, one launch (start us, length us, event | category | flops | bytes accessed | tf_op | source)
XLA Modules:
  0.0 103.7 jit_solution(11687999812376007540)
XLA Ops:
  0.6 0.0 copy-start.5
  0.6 0.0 copy-start.6
  0.7 0.6 copy-done.5
  1.3 0.0 copy-done.6
  1.3 0.0 copy-start
  1.3 1.0 %copy-done = bf16[1,1,512,512]{3,2,1,0:T(8,128)(2,1)S(1)} copy-done((bf16[1,1,512,512]{3,2,1,0:T(8,128)(2,1)S(1)}, bf16[1,1,512,512]{3,2,1,0:T(8,128)(2,1)}, u32[]{:S(2)}) %copy-start) | copy-done | bytes 524312
  2.3 0.0 copy-start.1
  2.3 1.0 %copy-done.1 = bf16[1,1,512,512]{3,2,1,0:T(8,128)(2,1)S(1)} copy-done((bf16[1,1,512,512]{3,2,1,0:T(8,128)(2,1)S(1)}, bf16[1,1,512,512]{3,2,1,0:T(8,128)(2,1)}, u32[]{:S(2)}) %copy-start.1) | copy-done | bytes 524312
  3.4 0.0 copy-start.2
  3.4 0.9 copy-done.2
  4.3 0.0 copy-start.3
  4.3 0.9 copy-done.3
  5.3 0.0 copy-start.4
  5.3 0.9 copy-done.4
  6.2 95.3 %shard_map.94 = (bf16[2,512,128]{2,1,0:T(8,128)(2,1)S(1)}, bf16[2,512,128]{2,1,0:T(8,128)(2,1)S(1)}, bf16[2,128,512]{2,1,0:T(8,128)(2,1)S(1)}) custom-call(s32[2]{0:T(128)S(1)} %bitcast.5, s32[2]{0:T(128)S(1)} %copy-done.6, bf16[512,512]{1,0:T(8,128)(2,1)S(1)} %bitcast.3, bf16[512,512]{1,0:T(8,128)(2,1)S(1)} %bitcast.4, bf16[2,512,128]{2,1,0:T(8,128)(2,1)S(1)} %copy-done.2, ...), custom_call_target="tpu_custom_call" | custom-call | tf_op jit(solution)/shard_map/pallas_call | solution.py:453
  101.5 0.7 copy.13
  102.3 0.7 copy.14
  103.0 0.7 copy.15
Async XLA Ops:
  0.6 0.7 copy-start.5
  0.6 0.7 copy-start.6
  1.3 1.0 %copy-start = (bf16[1,1,512,512]{3,2,1,0:T(8,128)(2,1)S(1)}, bf16[1,1,512,512]{3,2,1,0:T(8,128)(2,1)}, u32[]{:S(2)}) copy-start(bf16[1,1,512,512]{3,2,1,0:T(8,128)(2,1)} %param.7) | copy-start | bytes 1572868
  2.3 1.0 %copy-start.1 = (bf16[1,1,512,512]{3,2,1,0:T(8,128)(2,1)S(1)}, bf16[1,1,512,512]{3,2,1,0:T(8,128)(2,1)}, u32[]{:S(2)}) copy-start(bf16[1,1,512,512]{3,2,1,0:T(8,128)(2,1)} %param.8) | copy-start | bytes 1572868
  3.4 0.9 copy-start.2
  4.3 0.9 copy-start.3
  5.3 0.9 copy-start.4

commit v2 on v1

--- a/solution.py
+++ b/solution.py
@@ -130,10 +130,12 @@
 def fused_kernel(
     exchange, experts, counts_ref, match_ref, tok_ref, grad_ref, gate_ref, up_ref, down_ref,
     out_gate, out_up, out_down,
-    tok_all, grad_all, gu_all, dn_all, old_gate, old_up, old_down,
+    tok_all, grad_all, gu_all, dn_all, own_gate, own_up, own_down, old_gate, old_up, old_down,
     acc_gu, acc_gh, pre, hid, gate_sel, up_sel,
     part_gu, part_dn, core_gu, core_dn, sum_gu, sum_dn, far_gu, far_dn,
-    z_send, z_recv, y_send, y_recv, w_send, w_recv, r_send, r_recv,
+    dn_end, hid_out, hid_in, hid_end, acc_end, gh_out, gh_in,
+    part_de, core_de, sum_de, far_de, done_de, got_de,
+    z_send, z_recv, y_send, y_recv, w_send, w_recv, r_send, r_recv, e_send, e_recv, l_sem,
 ):
     zs = lax.axis_size("hidden")
     h = lax.axis_index("hidden")
@@ -144,6 +146,11 @@
     blocks = rows // BLOCK
     near, far = flip(d, 1), flip(d, 2)
     cross = flip(near, 2)
+    middle = (h > 0) & (h < zs - 1)
+    border = (h == 0) | (h == zs - 1)
+    helper = 1 + (h // (zs - 1)) * (zs - 3)
+    end = (h - 1) * (zs - 1)
+    last = (zs - 2 - h) * (zs - 1)
 
     def remote(source, target, send, recv, where):
         return pltpu.make_async_remote_copy(
@@ -179,19 +186,21 @@
             {"hidden": to},
         )
 
-    def sends(way, step):
+    def sends(kind, way, step):
         if way == 0:
-            return (h + 1 < zs) & (h - step >= 0), h - step
-        return (h - 1 >= 0) & (h + step < zs), h + step
-
-    def takes(way, step):
+            return (h + 1 < zs - kind) & (h - step >= 0), h - step
+        return (h - 1 >= kind) & (h + step < zs), h + step
+
+    def takes(kind, way, step):
         if way == 0:
-            return h - 1 - step >= 0, h - 1 - step
-        return h + 1 + step < zs, h + 1 + step
-
-    def line_start(kind, step):
-        for way in (0, 1):
-            valid, slab = sends(way, step)
+            valid, slab = h - 1 - step >= 0, h - 1 - step
+        else:
+            valid, slab = h + 1 + step < zs, h + 1 + step
+        return (valid & middle) if kind else valid, slab
+
+    def line_start(kind, step, ways=(0, 1)):
+        for way in ways:
+            valid, slab = sends(kind, way, step)
 
             @pl.when(valid)
             def _():
@@ -199,21 +208,21 @@
 
     def line_finish(kind, step):
         for way in (0, 1):
-            valid, slab = sends(way, step)
+            valid, slab = sends(kind, way, step)
 
             @pl.when(valid)
             def _():
                 line(kind, way, step, slab).wait_send()
 
-    def line_take(kind, step):
-        for way in (0, 1):
-            valid, slab = takes(way, step)
+    def line_take(kind, step, ways=(0, 1)):
+        for way in ways:
+            valid, slab = takes(kind, way, step)
 
             @pl.when(valid)
             def _():
                 line(kind, way, step, slab).wait_recv()
         if step + 1 < zs - 1:
-            line_start(kind, step + 1)
+            line_start(kind, step + 1, ways)
 
     def swap(i):
         source = (gate_ref, up_ref, down_ref)[i]
@@ -222,14 +231,17 @@
 
     line_start(0, 0)
     if exchange:
-        swap(0).start()
-        swap(1).start()
-    line_start(1, 0)
-    if exchange:
-        swap(2).start()
-
-    tok_all[h] = tok_ref[...]
-    grad_all[h] = grad_ref[...]
+        for i in range(3):
+            swap(i).start()
+    local = [
+        pltpu.make_async_copy(source, target, l_sem.at[i])
+        for i, (source, target) in enumerate((
+            (gate_ref, own_gate), (up_ref, own_up), (down_ref, own_down),
+            (tok_ref, tok_all.at[h]), (grad_ref, grad_all.at[h]),
+        ))
+    ]
+    for copy in local:
+        copy.start()
 
     def chosen(own, other, e):
         if not exchange:
@@ -249,28 +261,57 @@
         ref = weights[kind].at[slab]
         remote(ref, ref, w_send.at[kind, i], w_recv.at[kind, i], {"dp": near}).wait_recv()
 
+    line_take(0, 0)
+    line_start(1, 0)
+    for copy in local:
+        copy.wait()
     if exchange:
         swap(0).wait_recv()
         swap(1).wait_recv()
     for e in range(experts):
-        gu_all[d, e, :, :width] = chosen(gate_ref, old_gate, e)
-        gu_all[d, e, :, width:] = chosen(up_ref, old_up, e)
+        gu_all[d, e, :, :width] = chosen(own_gate, old_gate, e)
+        gu_all[d, e, :, width:] = chosen(own_up, old_up, e)
     spread(0, 0).start()
     spread(0, 1).start()
-    line_take(0, 0)
     if exchange:
         swap(2).wait_recv()
     for e in range(experts):
-        dn_all[d, e * width : (e + 1) * width, :] = chosen(down_ref, old_down, e)
+        dn_all[d, e * width : (e + 1) * width, :] = chosen(own_down, old_down, e)
     spread(1, 0).start()
     spread(1, 1).start()
-    line_take(1, 0)
+    line_take(0, 1)
+
+    @pl.when(h == 1)
+    def _():
+        line(1, 0, 0, h - 1).wait_recv()
+        line(1, 0, 1, h - 1).start()
+
+    @pl.when(h == zs - 2)
+    def _():
+        line(1, 1, 0, h + 1).wait_recv()
+        line(1, 1, 1, h + 1).start()
+
     for kind in (0, 1):
         arrived(kind, 0)
         spread(kind, 2).start()
     for kind in (0, 1):
         arrived(kind, 1)
         arrived(kind, 2)
+
+    def lend(i, owner, to):
+        slab = owner + (i + 1) * (1 - 2 * (owner // (zs - 1)))
+        return remote(
+            dn_all.at[slab], dn_end.at[slab], e_send.at[i], e_recv.at[i], {"hidden": to}
+        )
+
+    hidden_out = remote(hid_out, hid_in, e_send.at[3], e_recv.at[3], {"hidden": helper})
+    grads_out = remote(gh_out, gh_in, e_send.at[4], e_recv.at[4], {"hidden": end})
+    down_out = remote(done_de, got_de, e_send.at[5], e_recv.at[5], {"hidden": end})
+
+    @pl.when(border)
+    def _():
+        for i in range(3):
+            lend(i, h, helper).start()
 
     def add_tokens(slab, first=False):
         @pl.loop(0, rows // TILE)
@@ -280,35 +321,30 @@
                 term = jnp.dot(tok_all[slab, part], gu_all[slab, e], preferred_element_type=jnp.float32)
                 acc_gu[e, part] = term if first else acc_gu[e, part] + term
 
-    def add_grads(slab, first=False):
+    def add_grads(slab, first=False, total=acc_gh, weight=dn_all):
         @pl.loop(0, rows // TILE)
         def _(i):
             part = pl.ds(pl.multiple_of(i * TILE, TILE), TILE)
             term = lax.dot_general(
-                grad_all[slab, part], dn_all[slab], (((1,), (1,)), ((), ())),
+                grad_all[slab, part], weight[slab], (((1,), (1,)), ((), ())),
                 preferred_element_type=jnp.float32,
             )
-            acc_gh[part] = term if first else acc_gh[part] + term
-
-    def add_step(kind, step):
+            total[part] = term if first else total[part] + term
+
+    def add_step(step):
         for way in (0, 1):
-            valid, slab = takes(way, step)
+            valid, slab = takes(0, way, step)
 
             @pl.when(valid)
             def _():
-                (add_tokens, add_grads)[kind](slab)
+                add_tokens(slab)
 
     add_tokens(h, True)
     add_grads(h, True)
-    add_step(0, 0)
-    add_step(1, 0)
-    for step in range(1, zs - 2):
-        line_take(0, step)
-        add_step(0, step)
-        line_take(1, step)
-        add_step(1, step)
+    add_step(0)
+    add_step(1)
     line_take(0, zs - 2)
-    add_step(0, zs - 2)
+    add_step(zs - 2)
 
     bounds = [counts_ref[0]]
     for e in range(1, experts):
@@ -329,28 +365,36 @@
         gate_value, up_value = both[:, :width], both[:, width:]
         gate_sel[part] = gate_value
         up_sel[part] = up_value
-        hidden = (gate_value * jax.nn.sigmoid(gate_value) * up_value)
+        hidden = gate_value * jax.nn.sigmoid(gate_value) * up_value
+        hid_out[part] = (hidden * sum(masks[b])).astype(jnp.bfloat16)
         for e in range(experts):
             hid[part, e * width : (e + 1) * width] = (hidden * masks[b][e]).astype(jnp.bfloat16)
 
-    line_take(1, zs - 2)
-    add_step(1, zs - 2)
+    @pl.when(border)
+    def _():
+        hidden_out.start()
+
+    parts = (part_gu, part_dn, part_de)
+    cores = (core_gu, core_dn, core_de)
+    sums = (sum_gu, sum_dn, sum_de)
+    fars = (far_gu, far_dn, far_de)
 
     def reduce_near(kind, i):
         slab = (cross, near)[i]
-        source = (part_gu, part_dn)[kind].at[slab]
-        target = (core_gu, core_dn)[kind].at[i]
-        return remote(source, target, r_send.at[kind, i], r_recv.at[kind, i], {"dp": near})
+        return remote(
+            parts[kind].at[slab], cores[kind].at[i], r_send.at[kind, i], r_recv.at[kind, i],
+            {"dp": near},
+        )
 
     def reduce_far(kind):
         return remote(
-            (sum_gu, sum_dn)[kind], (far_gu, far_dn)[kind], r_send.at[kind, 2], r_recv.at[kind, 2],
-            {"dp": far},
+            sums[kind], fars[kind], r_send.at[kind, 2], r_recv.at[kind, 2], {"dp": far}
         )
 
-    def down_term(slab):
-        part_dn[slab] = lax.dot_general(
-            hid[...], grad_all[slab], (((0,), (0,)), ((), ())), preferred_element_type=jnp.float32
+    def down_term(kind, slab):
+        left = hid if kind == 1 else hid_end
+        parts[kind][slab] = lax.dot_general(
+            left[...], grad_all[slab], (((0,), (0,)), ((), ())), preferred_element_type=jnp.float32
         ).astype(jnp.bfloat16)
 
     def gate_term(slab):
@@ -363,29 +407,88 @@
             ).astype(jnp.bfloat16)
 
     def add_near(kind, i, slab):
-        own = (part_gu, part_dn)[kind]
-        got = (core_gu, core_dn)[kind]
-        return own[slab].astype(jnp.float32) + got[i].astype(jnp.float32)
-
-    def down_first():
-        down_term(cross)
-        reduce_near(1, 0).start()
-        down_term(far)
-        reduce_near(1, 0).wait_recv()
-        sum_dn[...] = add_near(1, 0, far).astype(jnp.bfloat16)
-        reduce_far(1).start()
-
-    def down_rest():
-        down_term(near)
-        reduce_near(1, 1).start()
-        down_term(d)
+        return parts[kind][slab].astype(jnp.float32) + cores[kind][i].astype(jnp.float32)
+
+    def down_phase(kind, late):
+        def at_turn(slab):
+            return pl.when(slab == last if late else slab != last)
+
+        @at_turn(cross)
+        def _():
+            down_term(kind, cross)
+            reduce_near(kind, 0).start()
+
+        @at_turn(far)
+        def _():
+            down_term(kind, far)
+            reduce_near(kind, 0).wait_recv()
+            sums[kind][...] = add_near(kind, 0, far).astype(jnp.bfloat16)
+            reduce_far(kind).start()
+
+        @at_turn(near)
+        def _():
+            down_term(kind, near)
+            reduce_near(kind, 1).start()
+
+        @at_turn(d)
+        def _():
+            down_term(kind, d)
+
+    @pl.when(middle)
+    def _():
+        @pl.when(h == 1)
+        def _():
+            line(1, 1, 0, h + 1).wait_recv()
+
+        @pl.when(h == zs - 2)
+        def _():
+            line(1, 0, 0, h - 1).wait_recv()
+
+        add_grads(h - 1)
+        add_grads(h + 1)
+        down_phase(1, False)
+        for i in range(3):
+            lend(i, end, helper).wait_recv()
+        add_grads(h, True, acc_end, dn_end)
+        add_grads(zs - 1 - h, False, acc_end, dn_end)
+        hidden_out.wait_recv()
+        for b in range(blocks):
+            part = slice(b * BLOCK, (b + 1) * BLOCK)
+            value = hid_in[part].astype(jnp.float32)
+            for e in range(experts):
+                hid_end[part, e * width : (e + 1) * width] = (value * masks[b][e]).astype(
+                    jnp.bfloat16
+                )
+        down_phase(2, False)
+
+        @pl.when(h == 1)
+        def _():
+            line(1, 1, 1, h + 2).wait_recv()
+
+        @pl.when(h == zs - 2)
+        def _():
+            line(1, 0, 1, h - 2).wait_recv()
+
+        add_grads(last, False, acc_end, dn_end)
+        for b in range(blocks):
+            part = slice(b * BLOCK, (b + 1) * BLOCK)
+            gh_out[part] = sum(
+                acc_end[part, e * width : (e + 1) * width] * picks[b][e] for e in range(experts)
+            ).astype(jnp.bfloat16)
+        grads_out.start()
+        add_grads(last)
+        gh_in[...] = jnp.zeros_like(gh_in)
+
+    @pl.when(border)
+    def _():
+        grads_out.wait_recv()
 
     for b in range(blocks):
         part = slice(b * BLOCK, (b + 1) * BLOCK)
         gate_value, up_value = gate_sel[part], up_sel[part]
         grad_hidden = sum(
             acc_gh[part, e * width : (e + 1) * width] * picks[b][e] for e in range(experts)
-        )
+        ) + gh_in[part].astype(jnp.float32)
         s = jax.nn.sigmoid(gate_value)
         grad_gate = grad_hidden * up_value * s * (1.0 + gate_value * (1.0 - s))
         grad_up = grad_hidden * gate_value * s
@@ -400,11 +503,23 @@
     reduce_near(0, 0).wait_recv()
     sum_gu[...] = add_near(0, 0, far).astype(jnp.bfloat16)
     reduce_far(0).start()
-    down_first()
     gate_term(near)
     reduce_near(0, 1).start()
+
+    @pl.when(middle)
+    def _():
+        down_phase(2, True)
+        down_phase(1, True)
+
     gate_term(d)
-    down_rest()
+
+    @pl.when(middle)
+    def _():
+        reduce_near(2, 1).wait_recv()
+        reduce_far(2).wait_recv()
+        total = add_near(2, 1, d) + far_de[...].astype(jnp.float32)
+        done_de[...] = total.astype(jnp.bfloat16)
+        down_out.start()
 
     reduce_near(0, 1).wait_recv()
     reduce_far(0).wait_recv()
@@ -413,20 +528,46 @@
         at = e * 2 * width
         out_gate[e] = total[:, at : at + width].astype(jnp.bfloat16)
         out_up[e] = total[:, at + width : at + 2 * width].astype(jnp.bfloat16)
-    reduce_near(1, 1).wait_recv()
-    reduce_far(1).wait_recv()
-    total = add_near(1, 1, d) + far_dn[...].astype(jnp.float32)
-    for e in range(experts):
-        out_down[e] = total[e * width : (e + 1) * width].astype(jnp.bfloat16)
+
+    @pl.when(middle)
+    def _():
+        reduce_near(1, 1).wait_recv()
+        reduce_far(1).wait_recv()
+        total = add_near(1, 1, d) + far_dn[...].astype(jnp.float32)
+        for e in range(experts):
+            out_down[e] = total[e * width : (e + 1) * width].astype(jnp.bfloat16)
+
+    @pl.when(border)
+    def _():
+        down_out.wait_recv()
+        for e in range(experts):
+            out_down[e] = got_de[e * width : (e + 1) * width]
+
+    def sent(kind):
+        for i in range(2):
+            reduce_near(kind, i).wait_send()
+        reduce_far(kind).wait_send()
 
     for kind in (0, 1):
         for step in range(zs - 1):
             line_finish(kind, step)
         for i in range(3):
             spread(kind, i).wait_send()
-        for i in range(2):
-            reduce_near(kind, i).wait_send()
-        reduce_far(kind).wait_send()
+    sent(0)
+
+    @pl.when(middle)
+    def _():
+        sent(1)
+        sent(2)
+        grads_out.wait_send()
+        down_out.wait_send()
+
+    @pl.when(border)
+    def _():
+        for i in range(3):
+            lend(i, h, helper).wait_send()
+        hidden_out.wait_send()
+
     if exchange:
         for i in range(3):
             swap(i).wait_send()
@@ -455,13 +596,16 @@
         out_shape=tuple(
             jax.ShapeDtypeStruct(w.shape, half) for w in (gate_weight, up_weight, down_weight)
         ),
-        in_specs=[smem, smem] + [vmem] * 5,
+        in_specs=[smem, smem] + [pl.BlockSpec(memory_space=pltpu.HBM)] * 5,
         out_specs=(vmem,) * 3,
         scratch_shapes=[
             pltpu.VMEM((zs, rows, feats), half),
             pltpu.VMEM((zs, rows, feats), half),
             pltpu.VMEM((ds, experts, part, 2 * width), half),
             pltpu.VMEM((ds, tall, part), half),
+            pltpu.VMEM(gate_weight.shape, half),
+            pltpu.VMEM(up_weight.shape, half),
+            pltpu.VMEM(down_weight.shape, half),
             pltpu.VMEM(gate_weight.shape, half),
             pltpu.VMEM(up_weight.shape, half),
             pltpu.VMEM(down_weight.shape, half),
@@ -479,17 +623,33 @@
             pltpu.VMEM((tall, part), half),
             pltpu.VMEM((part, wide), half),
             pltpu.VMEM((tall, part), half),
+            pltpu.VMEM((ds, tall, part), half),
+            pltpu.VMEM((rows, width), half),
+            pltpu.VMEM((rows, width), half),
+            pltpu.VMEM((rows, tall), half),
+            pltpu.VMEM((rows, tall), full),
+            pltpu.VMEM((rows, width), half),
+            pltpu.VMEM((rows, width), half),
+            pltpu.VMEM((ds, tall, part), half),
+            pltpu.VMEM((2, tall, part), half),
+            pltpu.VMEM((tall, part), half),
+            pltpu.VMEM((tall, part), half),
+            pltpu.VMEM((tall, part), half),
+            pltpu.VMEM((tall, part), half),
             dma((2, 2, zs - 1)),
             dma((2, 2, zs - 1)),
             dma((3,)),
             dma((3,)),
             dma((2, 3)),
             dma((2, 3)),
-            dma((2, 3)),
-            dma((2, 3)),
+            dma((3, 3)),
+            dma((3, 3)),
+            dma((6,)),
+            dma((6,)),
+            dma((5,)),
         ],
         compiler_params=pltpu.CompilerParams(
-            collective_id=0, has_side_effects=True, vmem_limit_bytes=48 * 1024 * 1024
+            collective_id=0, has_side_effects=True, vmem_limit_bytes=63 * 1024 * 1024
         ),
     )(
         block_counts.reshape(-1), matching, tokens.reshape(rows, feats),

time: 104 us -> 87.7 us (0.84)
  the two profiles are of different devices: /device:TPU:0 before, /device:TPU:7 now
where the time goes in v2:
time: 87.7 us; the launch traced here: 87.5 us
  Pallas kernels  83.4 us (95%)
  local copies, waits for them, and re-layouts  3.46 us (4%)
    pallas_call x1, Pallas kernels, on_device_fused(): pl.pallas_call(functools.partial(fused_kernel, exchange, experts), out_sh...  83.4 us
    unnamed x7, local copies, waits for them, and re-layouts  3.46 us

profile of v2, /device:TPU:7, one launch (start us, length us, event | category | flops | bytes accessed | tf_op | source)
XLA Modules:
  0.0 87.5 jit_solution(13646900338035119298)
XLA Ops:
  0.6 83.4 %shard_map.94 = (bf16[2,512,128]{2,1,0:T(8,128)(2,1)}, bf16[2,512,128]{2,1,0:T(8,128)(2,1)}, bf16[2,128,512]{2,1,0:T(8,128)(2,1)}) custom-call(s32[2]{0:T(128)} %bitcast.5, s32[2]{0:T(128)} %match_ref.1, bf16[512,512]{1,0:T(8,128)(2,1)} %bitcast.3, bf16[512,512]{1,0:T(8,128)(2,1)} %bitcast.4, bf16[2,512,128]{2,1,0:T(8,128)(2,1)} %gate_ref.1, ...), custom_call_target="tpu_custom_call" | custom-call | tf_op jit(solution)/shard_map/pallas_call | solution.py:594
  84.0 0.0 copy-start.1
  84.0 1.7 %copy.13 = bf16[2,512,128]{2,1,0:T(8,128)(2,1)} copy(bf16[2,512,128]{2,1,0:T(8,128)(2,1)} %get-tuple-element.6) | data formatting | bytes 524288
  85.7 0.0 copy-done.1
  85.7 0.0 copy-start
  85.7 0.7 copy.14
  86.4 0.3 copy-done
  86.8 0.7 copy.15
Async XLA Ops:
  84.0 1.7 %copy-start.1 = (bf16[2,512,128]{2,1,0:T(8,128)(2,1)S(1)}, bf16[2,512,128]{2,1,0:T(8,128)(2,1)}, u32[]{:S(2)}) copy-start(bf16[2,512,128]{2,1,0:T(8,128)(2,1)} %get-tuple-element.7) | copy-start | bytes 786436
  85.7 1.0 %copy-start = (bf16[2,128,512]{2,1,0:T(8,128)(2,1)S(1)}, bf16[2,128,512]{2,1,0:T(8,128)(2,1)}, u32[]{:S(2)}) copy-start(bf16[2,128,512]{2,1,0:T(8,128)(2,1)} %get-tuple-element.8) | copy-start | bytes 786436

commit v3 on v2

--- a/solution.py
+++ b/solution.py
@@ -476,6 +476,7 @@
                 acc_end[part, e * width : (e + 1) * width] * picks[b][e] for e in range(experts)
             ).astype(jnp.bfloat16)
         grads_out.start()
+        down_phase(2, True)
         add_grads(last)
         gh_in[...] = jnp.zeros_like(gh_in)
 
@@ -508,7 +509,6 @@
 
     @pl.when(middle)
     def _():
-        down_phase(2, True)
         down_phase(1, True)
 
     gate_term(d)

time: 87.7 us -> 85.4 us (0.974)
  the two profiles are of different devices: /device:TPU:7 before, /device:TPU:0 now
where the time goes in v3:
time: 85.4 us; the launch traced here: 84.9 us
  Pallas kernels  80.8 us (95%)
  local copies, waits for them, and re-layouts  3.46 us (4%)
    pallas_call x1, Pallas kernels, on_device_fused(): pl.pallas_call(functools.partial(fused_kernel, exchange, experts), out_sh...  80.8 us
    unnamed x7, local copies, waits for them, and re-layouts  3.46 us

profile of v3, /device:TPU:0, one launch (start us, length us, event | category | flops | bytes accessed | tf_op | source)
XLA Modules:
  0.0 84.9 jit_solution(4096582874256452769)
XLA Ops:
  0.6 80.8 %shard_map.94 = (bf16[2,512,128]{2,1,0:T(8,128)(2,1)}, bf16[2,512,128]{2,1,0:T(8,128)(2,1)}, bf16[2,128,512]{2,1,0:T(8,128)(2,1)}) custom-call(s32[2]{0:T(128)} %bitcast.5, s32[2]{0:T(128)} %match_ref.1, bf16[512,512]{1,0:T(8,128)(2,1)} %bitcast.3, bf16[512,512]{1,0:T(8,128)(2,1)} %bitcast.4, bf16[2,512,128]{2,1,0:T(8,128)(2,1)} %gate_ref.1, ...), custom_call_target="tpu_custom_call" | custom-call | tf_op jit(solution)/shard_map/pallas_call | solution.py:594
  81.4 0.0 copy-start.1
  81.4 1.7 %copy.13 = bf16[2,512,128]{2,1,0:T(8,128)(2,1)} copy(bf16[2,512,128]{2,1,0:T(8,128)(2,1)} %get-tuple-element.6) | data formatting | bytes 524288
  83.1 0.0 copy-done.1
  83.1 0.0 copy-start
  83.1 0.7 copy.14
  83.8 0.3 copy-done
  84.2 0.7 copy.15
Async XLA Ops:
  81.4 1.7 %copy-start.1 = (bf16[2,512,128]{2,1,0:T(8,128)(2,1)S(1)}, bf16[2,512,128]{2,1,0:T(8,128)(2,1)}, u32[]{:S(2)}) copy-start(bf16[2,512,128]{2,1,0:T(8,128)(2,1)} %get-tuple-element.7) | copy-start | bytes 786436
  83.1 1.0 %copy-start = (bf16[2,128,512]{2,1,0:T(8,128)(2,1)S(1)}, bf16[2,128,512]{2,1,0:T(8,128)(2,1)}, u32[]{:S(2)}) copy-start(bf16[2,128,512]{2,1,0:T(8,128)(2,1)} %get-tuple-element.8) | copy-start | bytes 786436
